TPU v7x, 256 devices: a whole 4x4x8 slice. The times are simulated.
256 devices in a mesh: seq: 32 (over x, z), head: 8 (over y, core).
Axes of the slice: x: 4, y: 4, z: 8, core: 2. Of those that a mesh axis runs over, the one named last changes fastest.
Arguments:
- tokens: bfloat16 [32768, 3072], P(('seq', 'head')), may hold values from -150 to 150
- norm_gain: float32 [3072], replicated, may hold values from 0.1 to 1.9
- w_query: bfloat16 [3072, 3072], P(None, 'head'), may hold values from -0.15625 to 0.15625
- w_key: bfloat16 [3072, 1024], P(None, 'head'), may hold values from -0.15625 to 0.15625
- w_value: bfloat16 [3072, 1024], P(None, 'head'), may hold values from -0.109375 to 0.109375
- w_out: bfloat16 [3072, 3072], P('head'), may hold values from -1.5 to 1.5
- long_cache: bfloat16 [2, 32768, 1024], P(None, 'seq', 'head'), may hold values from -244 to 244
- short_cache: bfloat16 [2, 8192, 1024], P(None, 'seq', 'head'), may hold values from -244 to 244
- slot_owner: int32 [8192], P('seq'), may hold values from -1 to 63, as said below
- new_len: int32 [64], replicated, may hold values from 2 to 1024, as said below
- cache_len: int32 [64], replicated, may hold values from 32 to 85, as said below
Outputs:
- layer_out: bfloat16 [32768, 3072], P(('seq', 'head'))
Inputs may be any that keep to these rules, and one draw needn't show every extreme that they name: `new_len`: lengths in order after the lead request's 64 tokens; they sum to 32704, and one request has exactly 1024 new tokens. `cache_len`: equals the number of short-cache slots that the request owns; one request has exactly 85. `slot_owner`: A request's slots are contiguous and lie in the block of 256 slots whose index equals that of the block of 1024 tokens holding the request's first new token.
All inputs are finite; a program needn't handle non-finite values.
Results may differ from a plain program's by a relative error of at most 0.02.
The roundings to bfloat16 on the way count: a program that leaves them out, or rounds other values in their place, can miss the bound.
Values may be sent and summed in bfloat16 or wider, within the bound.
A program may use at most 128 MiB of HBM per device.

v0:
```python
import math
import jax
import jax.numpy as jnp
from jax import lax
from jax.sharding import PartitionSpec as P

HD = 128
LEAD = 64
THETA_LOG = math.log(500000.0)


def from_behind(block, axis, distance):
    devices = range(lax.axis_size(axis))
    route = [(i - distance, i) for i in devices if i - distance in devices]
    return lax.ppermute(block, axis, route)


def rotate(field, position):
    half = field.shape[-1] // 2
    frequency = jnp.exp(jnp.arange(half, dtype=jnp.float32) * (-2.0 * THETA_LOG / field.shape[-1]))
    angle = position.astype(jnp.float32)[:, None] * frequency[None, :]
    cosine = jnp.cos(angle)[:, None, :]
    sine_part = jnp.sin(angle)[:, None, :]
    first_half = field[..., :half]
    second_half = field[..., half:]
    return jnp.concatenate(
        [
            first_half * cosine - second_half * sine_part,
            second_half * cosine + first_half * sine_part,
        ],
        axis=-1,
    )


def request_starts(new_len):
    return LEAD + jnp.cumsum(new_len) - new_len


def request_of(position_index, starts):
    passed = (starts[None, :] <= position_index[:, None]).astype(jnp.int32)
    request = jnp.sum(passed, axis=1) - 1
    return jnp.where(request < 0, starts.shape[0], request)


def position_of(position_index, request, starts, cache_len, long_len):
    number = starts.shape[0]
    select = jnp.arange(number, dtype=jnp.int32)[None, :] == request[:, None]
    begin = jnp.sum(jnp.where(select, starts[None, :], 0), axis=1)
    cached = jnp.sum(jnp.where(select, cache_len[None, :], 0), axis=1)
    return jnp.where(request == number, position_index + long_len, position_index - begin + cached)


def normalize(tokens, norm_gain):
    values = tokens.astype(jnp.float32)
    mean_square = jnp.mean(values * values, axis=-1, keepdims=True)
    return (values * lax.rsqrt(mean_square + 1e-05) * norm_gain).astype(jnp.bfloat16)


def raw_scores(queries, keys):
    return jnp.einsum("bgph,ngh->bgpn", queries, keys, preferred_element_type=jnp.float32) * (
        1.0 / math.sqrt(keys.shape[-1])
    )


def finish_state(scores, values):
    highest = jnp.max(scores, axis=-1)
    weights = jnp.exp(scores - highest[..., None])
    summed = jnp.sum(weights, axis=-1)
    mixture = jnp.einsum(
        "bgpn,ngh->bgph", weights.astype(jnp.bfloat16), values, preferred_element_type=jnp.float32
    )
    return (highest, summed, mixture)


def masked_state(queries, keys, values, valid):
    scores = jnp.where(valid[:, None, None, :], raw_scores(queries, keys), -jnp.inf)
    return finish_state(scores, values)


def plain_state(queries, keys, values):
    return finish_state(raw_scores(queries, keys), values)


def combine(former, latter):
    highest = jnp.maximum(former[0], latter[0])
    scale_former = jnp.exp(former[0] - highest)
    scale_latter = jnp.exp(latter[0] - highest)
    summed = former[1] * scale_former + latter[1] * scale_latter
    mixture = former[2] * scale_former[..., None] + latter[2] * scale_latter[..., None]
    return (highest, summed, mixture)


def on_device(
    tokens,
    norm_gain,
    w_query,
    w_key,
    w_value,
    w_out,
    long_cache,
    short_cache,
    slot_owner,
    new_len,
    cache_len,
):
    seq_index = lax.axis_index("seq")
    long_len = long_cache.shape[1] * lax.axis_size("seq")
    kv_heads = w_key.shape[1] // HD
    q_heads = w_query.shape[1] // HD
    per_kv = q_heads // kv_heads
    slots = short_cache.shape[1]
    q_width = w_query.shape[1]
    k_width = w_key.shape[1]
    earlier_slots, earlier_owner = from_behind((short_cache, slot_owner), "seq", 1)
    normed = normalize(tokens, norm_gain)
    piece = lax.all_gather(normed, "head", axis=0, tiled=True)
    projected = jnp.concatenate(
        [
            jnp.dot(piece, w_query, preferred_element_type=jnp.float32),
            jnp.dot(piece, w_key, preferred_element_type=jnp.float32),
            jnp.dot(piece, w_value, preferred_element_type=jnp.float32),
        ],
        axis=1,
    )
    local_rows = projected.shape[0]
    starts = request_starts(new_len)
    token_index = seq_index * local_rows + jnp.arange(local_rows, dtype=jnp.int32)
    request = request_of(token_index, starts)
    position = position_of(token_index, request, starts, cache_len, long_len)
    before_index = token_index - local_rows
    before_request = request_of(before_index, starts)
    queries = rotate(projected[:, :q_width].reshape(local_rows, q_heads, HD), position).astype(
        jnp.bfloat16
    )
    queries = queries.reshape(local_rows, kv_heads, per_kv, HD)
    keys = rotate(
        projected[:, q_width : q_width + k_width].reshape(local_rows, kv_heads, HD), position
    ).astype(jnp.bfloat16)
    values = projected[:, q_width + k_width :].astype(jnp.bfloat16)
    fresh = jnp.stack([keys.reshape(local_rows, k_width), values])
    earlier_fresh = from_behind(fresh, "seq", 1)
    has_before = seq_index > 0
    new_rows = jnp.concatenate([earlier_fresh, fresh], axis=1)
    new_keys = new_rows[0].reshape(-1, kv_heads, HD)
    new_values = new_rows[1].reshape(-1, kv_heads, HD)
    slot_rows = jnp.concatenate([earlier_slots, short_cache], axis=1)
    slot_keys = slot_rows[0].reshape(-1, kv_heads, HD)
    slot_values = slot_rows[1].reshape(-1, kv_heads, HD)
    new_request = jnp.concatenate([jnp.where(has_before, before_request, -1), request])
    new_index = jnp.concatenate([before_index, token_index])
    slot_request = jnp.concatenate([jnp.where(has_before, earlier_owner, -1), slot_owner]).astype(
        jnp.int32
    )
    slot_index = jnp.full((2 * slots,), -1, jnp.int32)
    block_rows = min(local_rows, 512)
    block_count = local_rows // block_rows
    window = local_rows + block_rows

    def local_block(item):
        block_queries, block_request, block_index, block_number = item
        begin = block_number * block_rows
        window_keys = jnp.concatenate(
            [lax.dynamic_slice_in_dim(new_keys, begin, window, 0), slot_keys], axis=0
        )
        window_values = jnp.concatenate(
            [lax.dynamic_slice_in_dim(new_values, begin, window, 0), slot_values], axis=0
        )
        window_request = jnp.concatenate(
            [lax.dynamic_slice_in_dim(new_request, begin, window, 0), slot_request]
        )
        window_index = jnp.concatenate(
            [lax.dynamic_slice_in_dim(new_index, begin, window, 0), slot_index]
        )
        valid = (window_request[None, :] == block_request[:, None]) & (
            window_index[None, :] <= block_index[:, None]
        )
        return masked_state(block_queries, window_keys, window_values, valid)

    highest, summed, mixture = lax.map(
        local_block,
        (
            queries.reshape(block_count, block_rows, kv_heads, per_kv, HD),
            request.reshape(block_count, block_rows),
            token_index.reshape(block_count, block_rows),
            jnp.arange(block_count, dtype=jnp.int32),
        ),
    )
    highest = highest.reshape(local_rows, kv_heads, per_kv)
    summed = summed.reshape(local_rows, kv_heads, per_kv)
    mixture = mixture.reshape(local_rows, kv_heads, per_kv, HD)
    lead_queries = queries[:LEAD]
    start_state = (
        jnp.full((LEAD, kv_heads, per_kv), -1e30, jnp.float32),
        jnp.zeros((LEAD, kv_heads, per_kv), jnp.float32),
        jnp.zeros((LEAD, kv_heads, per_kv, HD), jnp.float32),
    )
    piece = lax.all_gather(long_cache, "seq", axis=1, tiled=True)
    long_state = combine(
        start_state,
        plain_state(
            lead_queries, piece[0].reshape(-1, kv_heads, HD), piece[1].reshape(-1, kv_heads, HD)
        ),
    )
    long_highest = jnp.where(seq_index == 0, long_state[0], -1e30)
    joined = combine(
        (highest[:LEAD], summed[:LEAD], mixture[:LEAD]),
        (long_highest, long_state[1], long_state[2]),
    )
    summed = jnp.concatenate([joined[1], summed[LEAD:]], axis=0)
    mixture = jnp.concatenate([joined[2], mixture[LEAD:]], axis=0)
    attended = (mixture / summed[..., None]).astype(jnp.bfloat16).reshape(local_rows, q_width)
    gathered_sum = lax.psum_scatter(
        jnp.dot(attended, w_out, preferred_element_type=jnp.float32).astype(jnp.bfloat16),
        "head",
        scatter_dimension=0,
        tiled=True,
    )
    return gathered_sum


def solution(mesh):
    placed = (
        P(("seq", "head"), None),
        P(),
        P(None, "head"),
        P(None, "head"),
        P(None, "head"),
        P("head", None),
        P(None, "seq", "head"),
        P(None, "seq", "head"),
        P("seq"),
        P(),
        P(),
    )
    return jax.shard_map(
        on_device, mesh=mesh, in_specs=placed, out_specs=P(("seq", "head"), None), check_vma=False
    )
```

profile of v0, /device:TPU:1, one launch (start us, length us, event | category | flops | bytes accessed | tf_op | source)
XLA Modules:
  0.0 298.3 jit_solution(11702035966844528671)
XLA Ops:
  8.1 2.3 fusion.31
  11.2 4.4 %collective-permute-start = (s32[256]{0:T(256)}, s32[256]{0:T(256)S(1)}, u32[]{:S(2)}, u32[]{:S(2)}) collective-permute-start(s32[256]{0:T(256)} %param.21), channel_id=1, source_target_pairs={{0,8},{8,16},{16,24},{24,32},{32,40},{40,48},{48,56},{56,64},{64,7... | collective-permute-start | bytes 3080 | tf_op jit(solution)/shard_map/ppermute | solution.py:15
  15.6 3.6 %collective-permute-start.2 = (bf16[2,256,128]{2,1,0:T(8,128)(2,1)}, bf16[2,256,128]{2,1,0:T(8,128)(2,1)S(1)}, u32[]{:S(2)}, u32[]{:S(2)}) collective-permute-start(bf16[2,256,128]{2,1,0:T(8,128)(2,1)} %param.20), channel_id=1, source_target_pairs={{0,8},{8,16},{16,24},{24,32},{32,40},{40,48},{48,56},{56,64},{64,7... | collective-permute-start | bytes 393224 | tf_op jit(solution)/shard_map/ppermute | solution.py:15
  22.4 3.1 %multiply_cosine_fusion = (f32[1024,64]{1,0:T(8,128)}, f32[1024,64]{1,0:T(8,128)}) fusion(f32[64]{0:T(128)S(1)} %multiply_exponential_fusion, f32[1024]{0:T(1024)S(1)} %get-tuple-element.196), kind=kLoop, calls=%fused_computation.63 | loop fusion | flops 65536 | bytes 528640 | tf_op jit(solution)/shard_map/cos | solution.py:22
  28.1 30.1 %all-gather.3.cloned.1.call-done = bf16[1024,3072]{1,0:T(8,128)(2,1)} async-done(((bf16[128,3072]{1,0:T(8,128)(2,1)}), bf16[1024,3072]{1,0:T(8,128)(2,1)}) %all-gather.3.cloned.1.call-update) | async-done | bytes 6291472 | tf_op jit(solution)/shard_map/all_gather | solution.py:116
  58.3 5.3 %convolution_bitcast_fusion = f32[1024,1,128]{0,2,1:T(8,128)S(1)} fusion(bf16[1024,3072]{1,0:T(8,128)(2,1)} %all-gather.3.cloned.1.call-done, bf16[3072,128]{1,0:T(8,128)(2,1)} %param.16), kind=kOutput, calls=%fused_computation.51 | convolution fusion | flops 805306368 | bytes 7602176 | tf_op jit(solution)/shard_map/dot_general | solution.py:120
  64.8 2.2 fusion.33
  67.9 4.0 %collective-permute-start.1 = (bf16[2,1024,128]{1,2,0:T(8,128)(2,1)}, bf16[2,1024,128]{1,2,0:T(8,128)(2,1)}, u32[]{:S(2)}, u32[]{:S(2)}) collective-permute-start(bf16[2,1024,128]{1,2,0:T(8,128)(2,1)} %pad_maximum_fusion.1), channel_id=1, source_target_pairs={{0,8},{8,16},{16,24},{24,32},{32,40},{40,48},{48,56},{56,64},{64,7... | collective-permute-start | bytes 1572872 | tf_op jit(solution)/shard_map/ppermute | solution.py:15
  71.9 2.7 fusion.76
  75.6 2.8 copy.74
  80.0 2.6 subtract_convert_fusion
  84.9 4.6 %collective-permute-done.1 = bf16[2,1024,128]{1,2,0:T(8,128)(2,1)} collective-permute-done((bf16[2,1024,128]{1,2,0:T(8,128)(2,1)}, bf16[2,1024,128]{1,2,0:T(8,128)(2,1)}, u32[]{:S(2)}, u32[]{:S(2)}) %collective-permute-start.1) | collective-permute-done | bytes 524320 | tf_op jit(solution)/shard_map/ppermute | solution.py:15
  91.7 73.2 %while.14 = (s32[]{:T(128)}, f32[2,512,1,3]{1,0,3,2:T(2,128)}, f32[2,512,1,3]{1,0,2,3:T(2,128)}, f32[2,512,1,3,128]{4,1,0,3,2:T(8,128)}, s32[2]{0:T(128)S(1)}, /...) while((s32[]{:T(128)}, f32[2,512,1,3]{1,0,3,2:T(2,128)}, ...), condition=%wide.region_9.10_spmd, body=%wide.region_6.9_spmd.sunk | while | flops 1650459648 | bytes 50030996 | solution.py:179
  96.2 2.1 constant_dynamic-slice_fusion.7
  98.2 1.9 copy.86
  100.2 8.1 %fusion.90 = (f32[512,3]{0,1:T(4,128)S(1)}, f32[2048,512,3]{1,0,2:T(8,128)}) fusion(pred[512,2048]{0,1:T(8,128)(4,1)S(1)} %compare_and_fusion.2, bf16[2,512,1,3,128]{4,1,0,3,2:T(8,128)(2,1)} %get-tuple-element.368, s32[]{:T(128)S(6)} %copy.97, bf16[512,1,128]{2,0,1:T(8,128)(2,1)} %get-tuple-element.367, bf16[1536,1,128]{2,0,1:T(8,128)(2,1)} %copy.86), kind=kOutput, calls=%fused_computation.4.clone.1 | convolution fusion | flops 815790592 | bytes 14555140 | tf_op jit(solution)/shard_map/while/body/eval_jaxpr/bgph,ngh->bgpn/dot_general | solution.py:60
  108.4 7.3 %fusion.91 = f32[512,3]{0,1:T(4,128)S(1)} fusion(f32[2048,512,3]{1,0,2:T(8,128)} %get-tuple-element.311, f32[512,3]{0,1:T(4,128)S(1)} %get-tuple-element.310, pred[512,2048]{0,1:T(8,128)(4,1)S(1)} %compare_and_fusion.2), kind=kLoop, calls=%fused_computation.3.clone.1 | loop fusion | flops 12581376 | bytes 13643776 | tf_op jit(solution)/shard_map/while/body/eval_jaxpr/reduce_sum | solution.py:68
  115.8 10.4 %fusion.92 = f32[1,512,1,3,128]{1,4,3,2,0:T(8,128)} fusion(f32[2048,512,3]{1,0,2:T(8,128)} %get-tuple-element.311, f32[512,3]{0,1:T(4,128)S(1)} %get-tuple-element.310, pred[512,2048]{0,1:T(8,128)(4,1)S(1)} %compare_and_fusion.2, bf16[512,1,128]{0,2,1:T(8,128)(2,1)} %get-tuple-element.370, bf16[1536,1,128]{0,2,1:T(8,128)(2,1)} %get-tuple-element.312), kind=kOutput, calls=%fused_computation.9.clone.1 | convolution fusion | flops 818937856 | bytes 14948352 | tf_op jit(solution)/shard_map/while/body/eval_jaxpr/bgpn,ngh->bgph/dot_general | solution.py:69
  133.0 2.1 constant_dynamic-slice_fusion.7
  135.1 1.9 copy.86
  137.0 8.1 %fusion.90 = (f32[512,3]{0,1:T(4,128)S(1)}, f32[2048,512,3]{1,0,2:T(8,128)}) fusion(pred[512,2048]{0,1:T(8,128)(4,1)S(1)} %compare_and_fusion.2, bf16[2,512,1,3,128]{4,1,0,3,2:T(8,128)(2,1)} %get-tuple-element.368, s32[]{:T(128)S(6)} %copy.97, bf16[512,1,128]{2,0,1:T(8,128)(2,1)} %get-tuple-element.367, bf16[1536,1,128]{2,0,1:T(8,128)(2,1)} %copy.86), kind=kOutput, calls=%fused_computation.4.clone.1 | convolution fusion | flops 815790592 | bytes 14555140 | tf_op jit(solution)/shard_map/while/body/eval_jaxpr/bgph,ngh->bgpn/dot_general | solution.py:60
  145.2 7.6 %fusion.91 = f32[512,3]{0,1:T(4,128)S(1)} fusion(f32[2048,512,3]{1,0,2:T(8,128)} %get-tuple-element.311, f32[512,3]{0,1:T(4,128)S(1)} %get-tuple-element.310, pred[512,2048]{0,1:T(8,128)(4,1)S(1)} %compare_and_fusion.2), kind=kLoop, calls=%fused_computation.3.clone.1 | loop fusion | flops 12581376 | bytes 13643776 | tf_op jit(solution)/shard_map/while/body/eval_jaxpr/reduce_sum | solution.py:68
  152.9 9.6 %fusion.92 = f32[1,512,1,3,128]{1,4,3,2,0:T(8,128)} fusion(f32[2048,512,3]{1,0,2:T(8,128)} %get-tuple-element.311, f32[512,3]{0,1:T(4,128)S(1)} %get-tuple-element.310, pred[512,2048]{0,1:T(8,128)(4,1)S(1)} %compare_and_fusion.2, bf16[512,1,128]{0,2,1:T(8,128)(2,1)} %get-tuple-element.370, bf16[1536,1,128]{0,2,1:T(8,128)(2,1)} %get-tuple-element.312), kind=kOutput, calls=%fused_computation.9.clone.1 | convolution fusion | flops 818937856 | bytes 14948352 | tf_op jit(solution)/shard_map/while/body/eval_jaxpr/bgpn,ngh->bgph/dot_general | solution.py:69
  164.9 2.7 slice.77
  167.6 3.1 %copy.54 = f32[960,1,3,128]{0,3,2,1:T(8,128)} copy(f32[960,1,3,128]{3,0,2,1:T(8,128)} %slice.77) | data formatting | bytes 2949120 | tf_op jit(solution)/shard_map/slice | solution.py:210
  170.8 33.9 %all-gather.5.cloned.1.call-done = bf16[2,32768,128]{2,1,0:T(8,128)(2,1)} async-done(((bf16[2,1024,128]{2,1,0:T(8,128)(2,1)}), bf16[2,32768,128]{2,1,0:T(8,128)(2,1)}) %all-gather.5.cloned.1.call-update) | async-done | bytes 16777232 | tf_op jit(solution)/shard_map/all_gather | solution.py:197
  204.8 12.3 %fusion.75 = (f32[64,3]{0,1:T(4,128)S(1)}, f32[64,1,3,32768]{3,0,2,1:T(8,128)}) fusion(bf16[2,32768,128]{2,1,0:T(8,128)(2,1)} %all-gather.5.cloned.1.call-done, bf16[1024,3,64]{2,0,1:T(8,128)(2,1)} %copy-done.4, bf16[1024,3,64]{2,0,1:T(8,128)(2,1)S(1)} %copy-done.3), kind=kOutput, calls=%fused_computation.124 | convolution fusion | flops 1623293696 | bytes 34734848 | tf_op jit(solution)/shard_map/bgph,ngh->bgpn/dot_general | solution.py:60
  217.0 10.6 %fusion.23 = f32[64,3]{0,1:T(4,128)S(1)} fusion(f32[64,1,3,32768]{3,0,2,1:T(8,128)} %get-tuple-element.201, f32[64,3]{0,1:T(4,128)S(1)} %get-tuple-element.200), kind=kLoop, calls=%fused_computation.34 | loop fusion | flops 12582720 | bytes 25167360 | tf_op jit(solution)/shard_map/reduce_sum | solution.py:68
  227.7 14.4 %fusion.49 = f32[64,1,3,128]{3,0,2,1:T(8,128)S(1)} fusion(bf16[2,32768,128]{2,1,0:T(8,128)(2,1)} %all-gather.5.cloned.1.call-done, f32[64,1,3,32768]{3,0,2,1:T(8,128)} %get-tuple-element.201, f32[64,3]{0,1:T(4,128)S(1)} %get-tuple-element.200, f32[1024,1,3,128]{3,0,2,1:T(8,128)} %bitcast.189, f32[64,3]{0,1:T(4,128)S(1)} %bitcast.196, ...), kind=kOutput, calls=%fused_computation.59 | convolution fusion | flops 1623318528 | bytes 33754880 | tf_op jit(solution)/shard_map/bgpn,ngh->bgph/dot_general | solution.py:69
  242.4 1.9 fusion.32
  244.3 5.4 %convolution_convert_fusion = bf16[1024,3072]{1,0:T(8,128)(2,1)} fusion(bf16[1024,384]{0,1:T(8,128)(2,1)S(1)} %fusion.32, bf16[384,3072]{1,0:T(8,128)(2,1)S(1)} %copy-done), kind=kOutput, calls=%fused_computation.41 | convolution fusion | flops 2419064832 | bytes 9437184 | tf_op jit(solution)/shard_map/dot_general | solution.py:213
  249.7 42.1 %reduce-scatter.2.cloned.1.call-done = bf16[128,3072]{1,0:T(8,128)(2,1)} async-done(((bf16[1024,3072]{1,0:T(8,128)(2,1)}), bf16[128,3072]{1,0:T(8,128)(2,1)}) %reduce-scatter.2.cloned.1.call-update) | async-done | bytes 786448 | tf_op jit(solution)/shard_map/reduce_scatter | solution.py:212
  (118 shorter events, 30.3 us)
Async XLA Ops:
  6.5 237.7 %copy-start = (bf16[384,3072]{1,0:T(8,128)(2,1)S(1)}, bf16[384,3072]{1,0:T(8,128)(2,1)}, u32[]{:S(2)}) copy-start(bf16[384,3072]{1,0:T(8,128)(2,1)} %param.18) | copy-start | bytes 7077892
  6.5 20.1 %copy-start.8 = (bf16[2,256,128]{2,1,0:T(8,128)(2,1)S(1)}, bf16[2,256,128]{2,1,0:T(8,128)(2,1)}, u32[]{:S(2)}) copy-start(bf16[2,256,128]{2,1,0:T(8,128)(2,1)} %param.20) | copy-start | bytes 393220
  6.5 51.7 %all-gather.3.cloned.1.call-start = ((), (), s32[]{:S(2)}) async-start(), calls=%async_computation.1 | async-start | bytes 7077888 | tf_op jit(solution)/shard_map/all_gather | solution.py:116
  10.4 194.4 %all-gather.5.cloned.1.call-start = ((), (), s32[]{:S(2)}) async-start(), calls=%async_computation.2 | async-start | bytes 17301504 | tf_op jit(solution)/shard_map/all_gather | solution.py:197
  11.1 280.7 %reduce-scatter.2.cloned.1.call-start = ((), (), s32[]{:S(2)}) async-start(), calls=%async_computation.3 | async-start | bytes 7077888 | tf_op jit(solution)/shard_map/reduce_scatter | solution.py:212
  11.2 14.8 %collective-permute-start = (s32[256]{0:T(256)}, s32[256]{0:T(256)S(1)}, u32[]{:S(2)}, u32[]{:S(2)}) collective-permute-start(s32[256]{0:T(256)} %param.21), channel_id=1, source_target_pairs={{0,8},{8,16},{16,24},{24,32},{32,40},{40,48},{48,56},{56,64},{64,7... | collective-permute-start | bytes 3080 | tf_op jit(solution)/shard_map/ppermute | solution.py:15
  15.6 11.1 %collective-permute-start.2 = (bf16[2,256,128]{2,1,0:T(8,128)(2,1)}, bf16[2,256,128]{2,1,0:T(8,128)(2,1)S(1)}, u32[]{:S(2)}, u32[]{:S(2)}) collective-permute-start(bf16[2,256,128]{2,1,0:T(8,128)(2,1)} %param.20), channel_id=1, source_target_pairs={{0,8},{8,16},{16,24},{24,32},{32,40},{40,48},{48,56},{56,64},{64,7... | collective-permute-start | bytes 393224 | tf_op jit(solution)/shard_map/ppermute | solution.py:15
  28.1 36.6 %copy-start.7 = (bf16[3072,128]{1,0:T(8,128)(2,1)S(1)}, bf16[3072,128]{1,0:T(8,128)(2,1)}, u32[]{:S(2)}) copy-start(bf16[3072,128]{1,0:T(8,128)(2,1)} %param.17) | copy-start | bytes 2359300
  58.3 6.5 %copy-start.1 = (bf16[1024,3072]{1,0:T(8,128)(2,1)S(1)}, bf16[1024,3072]{1,0:T(8,128)(2,1)}, u32[]{:S(2)}) copy-start(bf16[1024,3072]{1,0:T(8,128)(2,1)} %all-gather.3.cloned.1.call-done) | copy-start | bytes 18874372
  64.8 2.2 copy-start.5
  64.8 7.1 %copy-start.15 = (bf16[3072,384]{1,0:T(8,128)(2,1)S(1)}, bf16[3072,384]{1,0:T(8,128)(2,1)}, u32[]{:S(2)}) copy-start(bf16[3072,384]{1,0:T(8,128)(2,1)} %param.15) | copy-start | bytes 7077892
  67.9 21.6 %collective-permute-start.1 = (bf16[2,1024,128]{1,2,0:T(8,128)(2,1)}, bf16[2,1024,128]{1,2,0:T(8,128)(2,1)}, u32[]{:S(2)}, u32[]{:S(2)}) collective-permute-start(bf16[2,1024,128]{1,2,0:T(8,128)(2,1)} %pad_maximum_fusion.1), channel_id=1, source_target_pairs={{0,8},{8,16},{16,24},{24,32},{32,40},{40,48},{48,56},{56,64},{64,7... | collective-permute-start | bytes 1572872 | tf_op jit(solution)/shard_map/ppermute | solution.py:15
  80.0 9.5 %copy-start.6 = (bf16[1,1024,64]{1,2,0:T(8,128)(2,1)S(1)}, bf16[1,1024,64]{1,2,0:T(8,128)(2,1)}, u32[]{:S(2)}) copy-start(bf16[1,1024,64]{1,2,0:T(8,128)(2,1)} %copy-done.5) | copy-start | bytes 393220
  82.6 0.9 copy-start.2
  82.6 2.2 copy-start.4
  100.2 8.1 %copy-start.9 = (f32[2,512,1,3]{1,0,3,2:T(2,128)S(1)}, f32[2,512,1,3]{1,0,3,2:T(2,128)}, u32[]{:S(2)}) copy-start(f32[2,512,1,3]{1,0,3,2:T(2,128)} %get-tuple-element.335) | copy-start | bytes 36868 | tf_op jit(solution)/shard_map/while
  108.4 7.3 %copy-start.10 = (f32[2,512,1,3]{1,0,3,2:T(2,128)}, f32[2,512,1,3]{1,0,3,2:T(2,128)S(1)}, u32[]{:S(2)}) copy-start(f32[2,512,1,3]{1,0,3,2:T(2,128)S(1)} %dynamic_update_slice.16) | copy-start | bytes 36868 | tf_op jit(solution)/shard_map/while
  108.4 7.3 %copy-start.12 = (f32[2,512,1,3]{1,0,2,3:T(2,128)S(1)}, f32[2,512,1,3]{1,0,2,3:T(2,128)}, u32[]{:S(2)}) copy-start(f32[2,512,1,3]{1,0,2,3:T(2,128)} %get-tuple-element.336) | copy-start | bytes 36868 | tf_op jit(solution)/shard_map/while
  115.8 10.4 %copy-start.13 = (f32[2,512,1,3]{1,0,2,3:T(2,128)}, f32[2,512,1,3]{1,0,2,3:T(2,128)S(1)}, u32[]{:S(2)}) copy-start(f32[2,512,1,3]{1,0,2,3:T(2,128)S(1)} %dynamic_update_slice.17) | copy-start | bytes 36868 | tf_op jit(solution)/shard_map/while
  137.0 8.1 %copy-start.9 = (f32[2,512,1,3]{1,0,3,2:T(2,128)S(1)}, f32[2,512,1,3]{1,0,3,2:T(2,128)}, u32[]{:S(2)}) copy-start(f32[2,512,1,3]{1,0,3,2:T(2,128)} %get-tuple-element.335) | copy-start | bytes 36868 | tf_op jit(solution)/shard_map/while
  145.2 7.6 %copy-start.10 = (f32[2,512,1,3]{1,0,3,2:T(2,128)}, f32[2,512,1,3]{1,0,3,2:T(2,128)S(1)}, u32[]{:S(2)}) copy-start(f32[2,512,1,3]{1,0,3,2:T(2,128)S(1)} %dynamic_update_slice.16) | copy-start | bytes 36868 | tf_op jit(solution)/shard_map/while
  145.2 7.6 %copy-start.12 = (f32[2,512,1,3]{1,0,2,3:T(2,128)S(1)}, f32[2,512,1,3]{1,0,2,3:T(2,128)}, u32[]{:S(2)}) copy-start(f32[2,512,1,3]{1,0,2,3:T(2,128)} %get-tuple-element.336) | copy-start | bytes 36868 | tf_op jit(solution)/shard_map/while
  152.9 9.6 %copy-start.13 = (f32[2,512,1,3]{1,0,2,3:T(2,128)}, f32[2,512,1,3]{1,0,2,3:T(2,128)S(1)}, u32[]{:S(2)}) copy-start(f32[2,512,1,3]{1,0,2,3:T(2,128)S(1)} %dynamic_update_slice.17) | copy-start | bytes 36868 | tf_op jit(solution)/shard_map/while
  164.9 5.8 %copy-start.14 = (f32[2,512,1,3]{1,0,2,3:T(2,128)S(1)}, f32[2,512,1,3]{1,0,2,3:T(2,128)}, u32[]{:S(2)}) copy-start(f32[2,512,1,3]{1,0,2,3:T(2,128)} %get-tuple-element.91) | copy-start | bytes 36868
  164.9 5.8 %copy-start.11 = (f32[2,512,1,3]{1,0,3,2:T(2,128)S(1)}, f32[2,512,1,3]{1,0,3,2:T(2,128)}, u32[]{:S(2)}) copy-start(f32[2,512,1,3]{1,0,3,2:T(2,128)} %get-tuple-element.90) | copy-start | bytes 36868
  164.9 39.9 %copy-start.3 = (bf16[1024,3,64]{2,0,1:T(8,128)(2,1)S(1)}, bf16[1024,3,64]{2,0,1:T(8,128)(2,1)}, u32[]{:S(2)}) copy-start(bf16[1024,3,64]{2,0,1:T(8,128)(2,1)} %copy-done.2) | copy-start | bytes 1179652
Sparse Core Ops, SparseCore 0:
  10.5 47.6 all-gather.2
  60.8 143.8 all-gather.4
  249.8 41.9 reduce-scatter.1
where the time goes:
time: 299 us; the launch traced here: 298 us
  waiting for transfers between devices  111 us (37%)
  matrix products  78.4 us (26%)
  other arithmetic  49.5 us (17%)
  local copies, waits for them, and re-layouts  31.9 us (11%)
  between operations  13.4 us (4%)
  starting transfers between devices  12 us (4%)
    reduce_scatter x1, waiting for transfers between devices, on_device(): lax.psum_scatter(jnp.dot(attended, w_out, preferred_element_type=jnp.floa...  42.1 us
    dot_general x3, matrix products, finish_state(): jnp.einsum('bgpn,ngh->bgph', weights.astype(jnp.bfloat16), values, prefer...  34.4 us
    all_gather x1, waiting for transfers between devices, on_device(): piece = lax.all_gather(long_cache, 'seq', axis=1, tiled=True)  33.9 us
    all_gather x1, waiting for transfers between devices, on_device(): piece = lax.all_gather(normed, 'head', axis=0, tiled=True)  30.1 us
    dot_general x3, matrix products, raw_scores(): jnp.einsum('bgph,ngh->bgpn', queries, keys, preferred_element_type=jnp.fl...  28.4 us
    reduce_sum x3, other arithmetic, finish_state(): summed = jnp.sum(weights, axis=-1)  25.5 us
    ppermute x3, starting transfers between devices, from_behind(): return lax.ppermute(block, axis, route)  11.9 us
  transfers between devices with their start and end apart: 6, of which 4 were waited for; matrix products, arithmetic and copies ran while one was open for 37% of the time, Pallas kernels for 0%

commit v1 on v0

--- a/solution.py
+++ b/solution.py
@@ -194,7 +194,9 @@
         jnp.zeros((LEAD, kv_heads, per_kv), jnp.float32),
         jnp.zeros((LEAD, kv_heads, per_kv, HD), jnp.float32),
     )
-    piece = lax.all_gather(long_cache, "seq", axis=1, tiled=True)
+    piece = jnp.concatenate(
+        lax.all_to_all(jnp.stack(lax.axis_size("seq") * [long_cache], 0), "seq", 0, 0), 1
+    )
     long_state = combine(
         start_state,
         plain_state(

time: 299 us -> 655 us (2.19)
  waiting for transfers between devices: 111 us -> 438 us
  local copies, waits for them, and re-layouts: 31.9 us -> 51 us
  starting transfers between devices: 12 us -> 23.3 us
    ppermute x3, waiting for transfers between devices: 4.59 us -> 378 us  [from_behind(): return lax.ppermute(block, axis, route)]
    all_gather x1 -> x0, waiting for transfers between devices: 33.9 us -> none  [on_device(): piece = lax.all_gather(long_cache, 'seq', axis=1, tiled=True)]
    all_gather x1, waiting for transfers between devices: 30.1 us -> 0.01 us  [on_device(): piece = lax.all_gather(normed, 'head', axis=0, tiled=True)]
    reduce_scatter x1, waiting for transfers between devices: 42.1 us -> 59.8 us  [on_device(): lax.psum_scatter(jnp.dot(attended, w_out, preferred_element_type=jnp.floa...]
    all_to_all x0 -> x1, starting transfers between devices: none -> 12.1 us  [on_device(): lax.all_to_all(jnp.stack(lax.axis_size('seq') * [long_cache], 0), 'seq',...]
    slice x0 -> x1, local copies, waits for them, and re-layouts: none -> 11.9 us  [on_device(): piece[0].reshape(-1, kv_heads, HD)]
  transfers between devices with their start and end apart: 6 -> 6, of which waited for: 4 -> 3; matrix products, arithmetic and copies ran while one was open for 37% -> 17% of each run, Pallas kernels for 0% -> 0%
where the time goes in v1:
time: 655 us; the launch traced here: 654 us
  waiting for transfers between devices  438 us (67%)
  matrix products  79.9 us (12%)
  local copies, waits for them, and re-layouts  51 us (8%)
  other arithmetic  46.3 us (7%)
  starting transfers between devices  23.3 us (4%)
  between operations  13.8 us (2%)
    ppermute x3, waiting for transfers between devices, from_behind(): return lax.ppermute(block, axis, route)  378 us
    reduce_scatter x1, waiting for transfers between devices, on_device(): lax.psum_scatter(jnp.dot(attended, w_out, preferred_element_type=jnp.floa...  59.8 us
    dot_general x3, matrix products, finish_state(): jnp.einsum('bgpn,ngh->bgph', weights.astype(jnp.bfloat16), values, prefer...  33 us
    dot_general x3, matrix products, raw_scores(): jnp.einsum('bgph,ngh->bgpn', queries, keys, preferred_element_type=jnp.fl...  31.1 us
    reduce_sum x3, other arithmetic, finish_state(): summed = jnp.sum(weights, axis=-1)  25.2 us
  transfers between devices with their start and end apart: 6, of which 3 were waited for; matrix products, arithmetic and copies ran while one was open for 17% of the time, Pallas kernels for 0%

profile of v1, /device:TPU:1, one launch (start us, length us, event | category | flops | bytes accessed | tf_op | source)
XLA Modules:
  0.0 653.9 jit_solution(5804633739221457527)
XLA Ops:
  6.5 7.1 %stack.8 = bf16[32,2,1024,128]{3,2,1,0:T(8,128)(2,1)} broadcast(bf16[2,1024,128]{2,1,0:T(8,128)(2,1)} %param.19), dimensions={1,2,3} | broadcast | bytes 17301504 | tf_op jit(solution)/shard_map/stack | solution.py:198
  13.7 12.1 %all-to-all-start = ((bf16[32,2,1024,128]{3,2,1,0:T(8,128)(2,1)}), bf16[32,2,1024,128]{3,2,1,0:T(8,128)(2,1)}, u32[]{:S(2)}, u32[]{:S(2)}) async-start(bf16[32,2,1024,128]{3,2,1,0:T(8,128)(2,1)} %stack.8), calls=%async_computation | async-start | bytes 33554432 | tf_op jit(solution)/shard_map/all_to_all | solution.py:198
  27.4 3.1 collective-permute-start
  30.5 3.1 collective-permute-start.2
  34.9 3.0 multiply_cosine_fusion
  38.5 376.0 %collective-permute-done = s32[256]{0:T(256)S(1)} collective-permute-done((s32[256]{0:T(256)}, s32[256]{0:T(256)S(1)}, u32[]{:S(2)}, u32[]{:S(2)}) %collective-permute-start) | collective-permute-done | bytes 1056 | tf_op jit(solution)/shard_map/ppermute | solution.py:15
  415.1 2.3 collective-permute-done.2
  418.9 5.3 convolution_bitcast_fusion
  424.2 2.0 fusion.61
  426.3 2.2 fusion.33
  429.3 4.9 collective-permute-start.1
  434.2 2.7 fusion.77
  438.0 2.7 copy.90
  442.3 2.6 subtract_convert_fusion
  449.3 71.0 %while.14 = (s32[]{:T(128)}, f32[2,512,1,3]{1,0,3,2:T(2,128)}, f32[2,512,1,3]{1,0,2,3:T(2,128)}, f32[2,512,1,3,128]{4,1,0,3,2:T(8,128)}, s32[2]{0:T(128)S(1)}, /...) while((s32[]{:T(128)}, f32[2,512,1,3]{1,0,3,2:T(2,128)}, ...), condition=%wide.region_9.10_spmd, body=%wide.region_6.9_spmd.sunk | while | flops 1650459648 | bytes 50030996 | solution.py:179
  453.7 2.1 constant_dynamic-slice_fusion.7
  455.7 1.9 copy.102
  457.6 8.0 %fusion.93 = (f32[512,3]{0,1:T(4,128)S(1)}, f32[2048,512,3]{1,0,2:T(8,128)}) fusion(pred[512,2048]{0,1:T(8,128)(4,1)S(1)} %compare_and_fusion.2, bf16[2,512,1,3,128]{4,1,0,3,2:T(8,128)(2,1)} %get-tuple-element.386, s32[]{:T(128)S(6)} %copy.113, bf16[512,1,128]{2,0,1:T(8,128)(2,1)} %get-tuple-element.385, bf16[1536,1,128]{2,0,1:T(8,128)(2,1)} %copy.102), kind=kOutput, calls=%fused_computation.4.clone.1 | convolution fusion | flops 815790592 | bytes 14555140 | tf_op jit(solution)/shard_map/while/body/eval_jaxpr/bgph,ngh->bgpn/dot_general | solution.py:60
  465.7 7.3 %fusion.94 = f32[512,3]{0,1:T(4,128)S(1)} fusion(f32[2048,512,3]{1,0,2:T(8,128)} %get-tuple-element.329, f32[512,3]{0,1:T(4,128)S(1)} %get-tuple-element.328, pred[512,2048]{0,1:T(8,128)(4,1)S(1)} %compare_and_fusion.2), kind=kLoop, calls=%fused_computation.3.clone.1 | loop fusion | flops 12581376 | bytes 13643776 | tf_op jit(solution)/shard_map/while/body/eval_jaxpr/reduce_sum | solution.py:68
  473.1 9.3 %fusion.95 = f32[1,512,1,3,128]{1,4,3,2,0:T(8,128)} fusion(f32[2048,512,3]{1,0,2:T(8,128)} %get-tuple-element.329, f32[512,3]{0,1:T(4,128)S(1)} %get-tuple-element.328, pred[512,2048]{0,1:T(8,128)(4,1)S(1)} %compare_and_fusion.2, bf16[512,1,128]{0,2,1:T(8,128)(2,1)} %get-tuple-element.388, bf16[1536,1,128]{0,2,1:T(8,128)(2,1)} %get-tuple-element.330), kind=kOutput, calls=%fused_computation.9.clone.1 | convolution fusion | flops 818937856 | bytes 14948352 | tf_op jit(solution)/shard_map/while/body/eval_jaxpr/bgpn,ngh->bgph/dot_general | solution.py:69
  489.1 2.1 constant_dynamic-slice_fusion.7
  493.1 8.0 %fusion.93 = (f32[512,3]{0,1:T(4,128)S(1)}, f32[2048,512,3]{1,0,2:T(8,128)}) fusion(pred[512,2048]{0,1:T(8,128)(4,1)S(1)} %compare_and_fusion.2, bf16[2,512,1,3,128]{4,1,0,3,2:T(8,128)(2,1)} %get-tuple-element.386, s32[]{:T(128)S(6)} %copy.113, bf16[512,1,128]{2,0,1:T(8,128)(2,1)} %get-tuple-element.385, bf16[1536,1,128]{2,0,1:T(8,128)(2,1)} %copy.102), kind=kOutput, calls=%fused_computation.4.clone.1 | convolution fusion | flops 815790592 | bytes 14555140 | tf_op jit(solution)/shard_map/while/body/eval_jaxpr/bgph,ngh->bgpn/dot_general | solution.py:60
  501.2 7.3 %fusion.94 = f32[512,3]{0,1:T(4,128)S(1)} fusion(f32[2048,512,3]{1,0,2:T(8,128)} %get-tuple-element.329, f32[512,3]{0,1:T(4,128)S(1)} %get-tuple-element.328, pred[512,2048]{0,1:T(8,128)(4,1)S(1)} %compare_and_fusion.2), kind=kLoop, calls=%fused_computation.3.clone.1 | loop fusion | flops 12581376 | bytes 13643776 | tf_op jit(solution)/shard_map/while/body/eval_jaxpr/reduce_sum | solution.py:68
  508.6 9.3 %fusion.95 = f32[1,512,1,3,128]{1,4,3,2,0:T(8,128)} fusion(f32[2048,512,3]{1,0,2:T(8,128)} %get-tuple-element.329, f32[512,3]{0,1:T(4,128)S(1)} %get-tuple-element.328, pred[512,2048]{0,1:T(8,128)(4,1)S(1)} %compare_and_fusion.2, bf16[512,1,128]{0,2,1:T(8,128)(2,1)} %get-tuple-element.388, bf16[1536,1,128]{0,2,1:T(8,128)(2,1)} %get-tuple-element.330), kind=kOutput, calls=%fused_computation.9.clone.1 | convolution fusion | flops 818937856 | bytes 14948352 | tf_op jit(solution)/shard_map/while/body/eval_jaxpr/bgpn,ngh->bgph/dot_general | solution.py:69
  520.3 2.6 slice.79
  522.9 3.0 copy.70
  527.5 11.9 %fusion.74 = (bf16[1,32,1024,128]{3,2,0,1:T(8,128)(2,1)}, bf16[1,32,1024,128]{3,2,0,1:T(8,128)(2,1)}) fusion(bf16[2,32,1024,128]{3,2,0,1:T(8,128)(2,1)} %bitcast.28), kind=kLoop, calls=%fused_computation.121 | loop fusion | bytes 33554432 | tf_op jit(solution)/shard_map/slice | solution.py:203
  539.3 15.2 %fusion.76 = (f32[64,3]{0,1:T(4,128)S(1)}, f32[64,1,3,32768]{3,0,2,1:T(8,128)}) fusion(bf16[32768,128,1]{1,0,2:T(8,128)(2,1)} %bitcast.173, bf16[1024,3,64]{2,0,1:T(8,128)(2,1)S(1)} %copy-done.5, bf16[1024,3,64]{2,0,1:T(8,128)(2,1)S(1)} %copy-done.3), kind=kOutput, calls=%fused_computation.123 | convolution fusion | flops 1623293696 | bytes 34341632 | tf_op jit(solution)/shard_map/bgph,ngh->bgpn/dot_general | solution.py:60
  554.5 10.6 %fusion.23 = f32[64,3]{0,1:T(4,128)S(1)} fusion(f32[64,1,3,32768]{3,0,2,1:T(8,128)} %get-tuple-element.219, f32[64,3]{0,1:T(4,128)S(1)} %get-tuple-element.218), kind=kLoop, calls=%fused_computation.34 | loop fusion | flops 12582720 | bytes 25167360 | tf_op jit(solution)/shard_map/reduce_sum | solution.py:68
  565.2 14.4 %fusion.49 = f32[64,1,3,128]{3,0,2,1:T(8,128)S(1)} fusion(bf16[32768,128,1]{1,0,2:T(8,128)(2,1)} %bitcast.172, f32[64,1,3,32768]{3,0,2,1:T(8,128)} %get-tuple-element.219, f32[64,3]{0,1:T(4,128)S(1)} %get-tuple-element.218, f32[1024,1,3,128]{3,0,2,1:T(8,128)} %bitcast.178, f32[64,3]{0,1:T(4,128)S(1)} %bitcast.185, f32[64,3]{0,1:T(4,128)S(1)} %get-tuple-element.217, ...), kind=kOutput, calls=%fused_computation.57 | convolution fusion | flops 1623318528 | bytes 33754880 | tf_op jit(solution)/shard_map/bgpn,ngh->bgph/dot_general | solution.py:69
  581.7 5.5 convolution_convert_fusion
  587.2 59.8 %reduce-scatter.2.cloned.1.call-done = bf16[128,3072]{1,0:T(8,128)(2,1)} async-done(((bf16[1024,3072]{1,0:T(8,128)(2,1)}), bf16[128,3072]{1,0:T(8,128)(2,1)}) %reduce-scatter.2.cloned.1.call-update) | async-done | bytes 786448 | tf_op jit(solution)/shard_map/reduce_scatter | solution.py:214
  (129 shorter events, 31.2 us)
Async XLA Ops:
  6.5 575.2 %copy-start = (bf16[384,3072]{1,0:T(8,128)(2,1)S(1)}, bf16[384,3072]{1,0:T(8,128)(2,1)}, u32[]{:S(2)}) copy-start(bf16[384,3072]{1,0:T(8,128)(2,1)} %param.18) | copy-start | bytes 7077892
  13.7 12.2 %copy-start.6 = (bf16[128,3072]{1,0:T(8,128)(2,1)S(1)}, bf16[128,3072]{1,0:T(8,128)(2,1)}, u32[]{:S(2)}) copy-start(bf16[128,3072]{1,0:T(8,128)(2,1)} %param.13) | copy-start | bytes 2359300
  13.7 12.5 %copy-start.12 = (f32[3072]{0:T(1024)S(1)}, f32[3072]{0:T(1024)}, u32[]{:S(2)}) copy-start(f32[3072]{0:T(1024)} %param.14) | copy-start | bytes 36868
  13.7 16.8 %copy-start.10 = (bf16[2,256,128]{2,1,0:T(8,128)(2,1)S(1)}, bf16[2,256,128]{2,1,0:T(8,128)(2,1)}, u32[]{:S(2)}) copy-start(bf16[2,256,128]{2,1,0:T(8,128)(2,1)} %param.20) | copy-start | bytes 393220
  13.7 19.9 %copy-start.18 = (s32[64]{0:T(128)S(1)}, s32[64]{0:T(128)}, u32[]{:S(2)}) copy-start(s32[64]{0:T(128)} %param.22) | copy-start | bytes 772
  13.7 20.3 %copy-start.19 = (s32[64]{0:T(128)S(1)}, s32[64]{0:T(128)}, u32[]{:S(2)}) copy-start(s32[64]{0:T(128)} %param.23) | copy-start | bytes 772
  13.7 513.7 %all-to-all-start = ((bf16[32,2,1024,128]{3,2,1,0:T(8,128)(2,1)}), bf16[32,2,1024,128]{3,2,1,0:T(8,128)(2,1)}, u32[]{:S(2)}, u32[]{:S(2)}) async-start(bf16[32,2,1024,128]{3,2,1,0:T(8,128)(2,1)} %stack.8), calls=%async_computation | async-start | bytes 33554432 | tf_op jit(solution)/shard_map/all_to_all | solution.py:198
  25.8 393.0 %all-gather.2.cloned.1.call-start = ((), (), s32[]{:S(2)}) async-start(), calls=%async_computation.2 | async-start | bytes 7077888 | tf_op jit(solution)/shard_map/all_gather | solution.py:116
  27.3 619.7 %reduce-scatter.2.cloned.1.call-start = ((), (), s32[]{:S(2)}) async-start(), calls=%async_computation.3 | async-start | bytes 7077888 | tf_op jit(solution)/shard_map/reduce_scatter | solution.py:214
  27.4 387.1 %collective-permute-start = (s32[256]{0:T(256)}, s32[256]{0:T(256)S(1)}, u32[]{:S(2)}, u32[]{:S(2)}) collective-permute-start(s32[256]{0:T(256)} %param.21), channel_id=1, source_target_pairs={{0,8},{8,16},{16,24},{24,32},{32,40},{40,48},{48,56},{56,64},{64,7... | collective-permute-start | bytes 3080 | tf_op jit(solution)/shard_map/ppermute | solution.py:15
  30.5 386.9 %collective-permute-start.2 = (bf16[2,256,128]{2,1,0:T(8,128)(2,1)S(1)}, bf16[2,256,128]{2,1,0:T(8,128)(2,1)S(1)}, u32[]{:S(2)}, u32[]{:S(2)}) collective-permute-start(bf16[2,256,128]{2,1,0:T(8,128)(2,1)S(1)} %copy-done.10), channel_id=1, source_target_pairs={{0,8},{8,16},{16,24},{24,32},{32,40},{40,48},{48,56},{56,64},{64,7... | collective-permute-start | bytes 393224 | tf_op jit(solution)/shard_map/ppermute | solution.py:15
  34.2 384.6 %copy-start.11 = (f32[1024]{0:T(1024)}, f32[1024]{0:T(1024)S(1)}, u32[]{:S(2)}) copy-start(f32[1024]{0:T(1024)S(1)} %get-tuple-element.214) | copy-start | bytes 12292
  34.3 384.6 %copy-start.17 = (f32[64]{0:T(128)}, f32[64]{0:T(128)S(1)}, u32[]{:S(2)}) copy-start(f32[64]{0:T(128)S(1)} %multiply_exponential_fusion) | copy-start | bytes 772
  417.4 8.8 %copy-start.9 = (bf16[3072,128]{1,0:T(8,128)(2,1)S(1)}, bf16[3072,128]{1,0:T(8,128)(2,1)}, u32[]{:S(2)}) copy-start(bf16[3072,128]{1,0:T(8,128)(2,1)} %param.17) | copy-start | bytes 2359300
  418.9 7.4 %copy-start.1 = (bf16[1024,3072]{1,0:T(8,128)(2,1)S(1)}, bf16[1024,3072]{1,0:T(8,128)(2,1)}, u32[]{:S(2)}) copy-start(bf16[1024,3072]{1,0:T(8,128)(2,1)} %all-gather.2.cloned.1.call-done) | copy-start | bytes 18874372
  424.2 10.0 %copy-start.20 = (bf16[3072,384]{1,0:T(8,128)(2,1)S(1)}, bf16[3072,384]{1,0:T(8,128)(2,1)}, u32[]{:S(2)}) copy-start(bf16[3072,384]{1,0:T(8,128)(2,1)} %param.15) | copy-start | bytes 7077892
  426.2 3.1 copy-start.7
  429.3 17.8 %collective-permute-start.1 = (bf16[2,1024,128]{1,2,0:T(8,128)(2,1)}, bf16[2,1024,128]{1,2,0:T(8,128)(2,1)}, u32[]{:S(2)}, u32[]{:S(2)}) collective-permute-start(bf16[2,1024,128]{1,2,0:T(8,128)(2,1)} %pad_maximum_fusion.1), channel_id=1, source_target_pairs={{0,8},{8,16},{16,24},{24,32},{32,40},{40,48},{48,56},{56,64},{64,7... | collective-permute-start | bytes 1572872 | tf_op jit(solution)/shard_map/ppermute | solution.py:15
  442.3 4.8 copy-start.8
  444.9 0.9 copy-start.2
  444.9 2.2 copy-start.4
  457.6 8.0 %copy-start.13 = (f32[2,512,1,3]{1,0,3,2:T(2,128)S(1)}, f32[2,512,1,3]{1,0,3,2:T(2,128)}, u32[]{:S(2)}) copy-start(f32[2,512,1,3]{1,0,3,2:T(2,128)} %get-tuple-element.353) | copy-start | bytes 36868 | tf_op jit(solution)/shard_map/while
  465.7 7.3 %copy-start.14 = (f32[2,512,1,3]{1,0,3,2:T(2,128)}, f32[2,512,1,3]{1,0,3,2:T(2,128)S(1)}, u32[]{:S(2)}) copy-start(f32[2,512,1,3]{1,0,3,2:T(2,128)S(1)} %dynamic_update_slice.16) | copy-start | bytes 36868 | tf_op jit(solution)/shard_map/while
  465.7 7.3 %copy-start.15 = (f32[2,512,1,3]{1,0,2,3:T(2,128)S(1)}, f32[2,512,1,3]{1,0,2,3:T(2,128)}, u32[]{:S(2)}) copy-start(f32[2,512,1,3]{1,0,2,3:T(2,128)} %get-tuple-element.354) | copy-start | bytes 36868 | tf_op jit(solution)/shard_map/while
  473.1 9.3 %copy-start.16 = (f32[2,512,1,3]{1,0,2,3:T(2,128)}, f32[2,512,1,3]{1,0,2,3:T(2,128)S(1)}, u32[]{:S(2)}) copy-start(f32[2,512,1,3]{1,0,2,3:T(2,128)S(1)} %dynamic_update_slice.17) | copy-start | bytes 36868 | tf_op jit(solution)/shard_map/while
  493.1 8.0 %copy-start.13 = (f32[2,512,1,3]{1,0,3,2:T(2,128)S(1)}, f32[2,512,1,3]{1,0,3,2:T(2,128)}, u32[]{:S(2)}) copy-start(f32[2,512,1,3]{1,0,3,2:T(2,128)} %get-tuple-element.353) | copy-start | bytes 36868 | tf_op jit(solution)/shard_map/while
  501.2 7.3 %copy-start.14 = (f32[2,512,1,3]{1,0,3,2:T(2,128)}, f32[2,512,1,3]{1,0,3,2:T(2,128)S(1)}, u32[]{:S(2)}) copy-start(f32[2,512,1,3]{1,0,3,2:T(2,128)S(1)} %dynamic_update_slice.16) | copy-start | bytes 36868 | tf_op jit(solution)/shard_map/while
  501.2 7.3 %copy-start.15 = (f32[2,512,1,3]{1,0,2,3:T(2,128)S(1)}, f32[2,512,1,3]{1,0,2,3:T(2,128)}, u32[]{:S(2)}) copy-start(f32[2,512,1,3]{1,0,2,3:T(2,128)} %get-tuple-element.354) | copy-start | bytes 36868 | tf_op jit(solution)/shard_map/while
  508.6 9.3 %copy-start.16 = (f32[2,512,1,3]{1,0,2,3:T(2,128)}, f32[2,512,1,3]{1,0,2,3:T(2,128)S(1)}, u32[]{:S(2)}) copy-start(f32[2,512,1,3]{1,0,2,3:T(2,128)S(1)} %dynamic_update_slice.17) | copy-start | bytes 36868 | tf_op jit(solution)/shard_map/while
  527.4 11.9 %copy-start.3 = (bf16[1024,3,64]{2,0,1:T(8,128)(2,1)S(1)}, bf16[1024,3,64]{2,0,1:T(8,128)(2,1)}, u32[]{:S(2)}) copy-start(bf16[1024,3,64]{2,0,1:T(8,128)(2,1)} %copy-done.2) | copy-start | bytes 1179652
  527.5 11.9 %copy-start.5 = (bf16[1024,3,64]{2,0,1:T(8,128)(2,1)S(1)}, bf16[1024,3,64]{2,0,1:T(8,128)(2,1)}, u32[]{:S(2)}) copy-start(bf16[1024,3,64]{2,0,1:T(8,128)(2,1)} %copy-done.4) | copy-start | bytes 1179652
Sparse Core Ops, SparseCore 0:
  28.5 45.5 all-gather.1
  587.4 59.6 reduce-scatter.1
